TPU v7x, 32 devices: a whole 2x2x4 slice. The times are simulated.
32 devices in a mesh: parts: 2 (over y), blk: 16 (over z, x, core).
Axes of the slice: x: 2, y: 2, z: 4, core: 2. Of those that a mesh axis runs over, the one named last changes fastest.
Arguments:
- series: bfloat16 [16, 192, 11264], P(None, None, 'blk'), may hold values from -24 to 24
- subject_ids: int32 [16], P('parts'), parts along dimension 0, may hold values from 0 to 15
- net_labels: int32 [16], replicated, may hold values from 0 to 6
Outputs:
- connectome: float32 [22528, 11264], P(('parts', 'blk')), parts along dimension 0
There are 2 independent parts, one for each index of `parts`. A program takes and returns all parts, laid end to end along the dimension named above; an argument that names none is the same for every part. Nothing has to cross between parts.
Inputs may be any that keep to these rules, and one draw needn't show every extreme that they name: `subject_ids`: indices into the pool; a subject may repeat.
All inputs are finite; a program needn't handle non-finite values.
Results may differ from a plain program's by a relative error of at most 0.00072.
Values may be sent and summed in bfloat16 or wider, within the bound.
A program may use at most 384 MiB of HBM per device.

v0:
```python
import jax
import jax.numpy as jnp
from jax import lax
from jax.sharding import PartitionSpec as P

BLOCK = 704


def normalize(chosen):
    values = chosen.astype(jnp.float32)
    center = values - jnp.mean(values, axis=1, keepdims=True)
    spread = jnp.mean(center * center, axis=1, keepdims=True)
    return (center / jnp.sqrt(spread + 1e-05)).astype(jnp.bfloat16)


def fisher_value(corr):
    clipped = jnp.clip(corr, -0.999, 0.999)
    return 0.5 * jnp.log((1.0 + clipped) / (1.0 - clipped))


def fisher_sum(left, right):
    frames = left.shape[1]
    total = jnp.zeros((left.shape[2], right.shape[2]), jnp.float32)
    for subject in range(left.shape[0]):
        corr = (
            lax.dot_general(
                left[subject],
                right[subject],
                (((0,), (0,)), ((), ())),
                preferred_element_type=jnp.float32,
            )
            / frames
        )
        total = total + fisher_value(corr)
    return total


def fisher_tile(left, right, left_labels, right_labels):
    same = left_labels[:, None] == right_labels[None, :]
    empty = jnp.zeros((left.shape[2], right.shape[2]), jnp.float32)
    total = lax.cond(jnp.any(same), lambda: fisher_sum(left, right), lambda: empty)
    return jnp.where(same, total, empty)


def on_device(series, subject_ids, net_labels):
    chosen = jnp.take(series, subject_ids, axis=0)
    normalized = normalize(chosen)
    rows = normalized.shape[2]
    index = lax.axis_index("blk")
    row_labels = jnp.repeat(net_labels, BLOCK)
    own_labels = lax.dynamic_slice_in_dim(row_labels, index * rows, rows)
    return fisher_tile(
        normalized, lax.all_gather(normalized, "blk", axis=2, tiled=True), own_labels, row_labels
    )


def solution(mesh):
    return jax.shard_map(
        on_device,
        mesh=mesh,
        in_specs=(P(None, None, "blk"), P("parts"), P()),
        out_specs=P(("parts", "blk"), None),
        check_vma=False,
    )
```

profile of v0, /device:TPU:7, one launch (start us, length us, event | category | flops | bytes accessed | tf_op | source)
XLA Modules:
  0.0 545.0 jit_solution(16135795936443792558)
XLA Ops:
  6.5 0.7 compare_and_fusion
  7.2 0.7 compare_select_fusion.1
  7.9 3.0 gather_fusion
  10.9 0.6 convert_reduce_fusion
  11.5 0.9 fusion.25
  12.4 2.2 fusion.26
  14.6 4.9 copy.6
  19.6 0.7 broadcast_in_dim.24
  20.3 0.1 reshape.22
  20.4 0.1 dynamic_slice.3
  20.5 0.6 copy-done.2
  21.1 4.8 compare_reduce_fusion
  26.6 221.6 %all-gather.2.cloned.1.call-done = bf16[8,192,11264]{1,0,2:T(8,128)(2,1)} async-done(((bf16[8,192,704]{1,0,2:T(8,128)(2,1)}), bf16[8,192,11264]{1,0,2:T(8,128)(2,1)}) %all-gather.2.cloned.1.call-update) | async-done | bytes 34603024 | tf_op jit(solution)/shard_map/all_gather | solution.py:53
  248.2 267.2 %conditional.1 = (f32[704,11264]{1,0:T(8,128)}) conditional(s32[]{:T(128)} %convert_element_type.9, () %tuple.11, (bf16[8,192,704]{2,1,0:T(8,128)(2,1)}, bf16[8,192,11264]{1,0,2:T(8,128)(2,1)}) %tuple.12), branch_computations={%region_3.4_spmd, %region_4.5_spmd} | conditional | flops 24741150720 | bytes 590610432 | solution.py:41
  248.2 56.2 %copy.7 = bf16[8,192,11264]{2,1,0:T(8,128)(2,1)} copy(bf16[8,192,11264]{1,0,2:T(8,128)(2,1)} %get-tuple-element.17) | data formatting | bytes 69206016 | tf_op jit(solution)/shard_map
  304.4 17.6 %fusion = f32[704,11264]{1,0:T(8,128)} fusion(bf16[8,192,11264]{2,1,0:T(8,128)(2,1)} %copy.7, bf16[8,192,704]{2,1,0:T(8,128)(2,1)S(1)} %copy-done), kind=kOutput, calls=%fused_computation.4 | convolution fusion | flops 3045064704 | bytes 36339712 | tf_op jit(solution)/shard_map/cond/branch_1_fun/dot_general | solution.py:26
  322.0 17.0 %fusion.1 = f32[704,11264]{1,0:T(8,128)} fusion(bf16[8,192,11264]{2,1,0:T(8,128)(2,1)} %copy.7, bf16[8,192,704]{2,1,0:T(8,128)(2,1)S(1)} %copy-done), kind=kOutput, calls=%fused_computation.6 | convolution fusion | flops 3045064704 | bytes 36339712 | tf_op jit(solution)/shard_map/cond/branch_1_fun/dot_general | solution.py:26
  339.0 17.2 %fusion.2 = f32[704,11264]{1,0:T(8,128)} fusion(bf16[8,192,11264]{2,1,0:T(8,128)(2,1)} %copy.7, bf16[8,192,704]{2,1,0:T(8,128)(2,1)S(1)} %copy-done), kind=kOutput, calls=%fused_computation.8 | convolution fusion | flops 3045064704 | bytes 36339712 | tf_op jit(solution)/shard_map/cond/branch_1_fun/dot_general | solution.py:26
  356.2 17.0 %fusion.3 = f32[704,11264]{1,0:T(8,128)} fusion(bf16[8,192,11264]{2,1,0:T(8,128)(2,1)} %copy.7, bf16[8,192,704]{2,1,0:T(8,128)(2,1)S(1)} %copy-done), kind=kOutput, calls=%fused_computation.10 | convolution fusion | flops 3045064704 | bytes 36339712 | tf_op jit(solution)/shard_map/cond/branch_1_fun/dot_general | solution.py:26
  373.2 17.0 %fusion.4 = f32[704,11264]{1,0:T(8,128)} fusion(bf16[8,192,11264]{2,1,0:T(8,128)(2,1)} %copy.7, bf16[8,192,704]{2,1,0:T(8,128)(2,1)S(1)} %copy-done), kind=kOutput, calls=%fused_computation.12 | convolution fusion | flops 3045064704 | bytes 36339712 | tf_op jit(solution)/shard_map/cond/branch_1_fun/dot_general | solution.py:26
  390.3 17.3 %fusion.5 = f32[704,11264]{1,0:T(8,128)} fusion(bf16[8,192,11264]{2,1,0:T(8,128)(2,1)} %copy.7, bf16[8,192,704]{2,1,0:T(8,128)(2,1)S(1)} %copy-done), kind=kOutput, calls=%fused_computation.14 | convolution fusion | flops 3045064704 | bytes 36339712 | tf_op jit(solution)/shard_map/cond/branch_1_fun/dot_general | solution.py:26
  407.5 17.0 %fusion.6 = f32[704,11264]{1,0:T(8,128)} fusion(bf16[8,192,11264]{2,1,0:T(8,128)(2,1)} %copy.7, bf16[8,192,704]{2,1,0:T(8,128)(2,1)S(1)} %copy-done), kind=kOutput, calls=%fused_computation.16 | convolution fusion | flops 3045064704 | bytes 36339712 | tf_op jit(solution)/shard_map/cond/branch_1_fun/dot_general | solution.py:26
  424.5 90.6 %add_multiply_fusion = f32[704,11264]{1,0:T(8,128)} fusion(f32[704,11264]{1,0:T(8,128)} %fusion, f32[704,11264]{1,0:T(8,128)} %fusion.1, f32[704,11264]{1,0:T(8,128)} %fusion.2, f32[704,11264]{1,0:T(8,128)} %fusion.3, f32[704,11264]{1,0:T(8,128)} %fusion.4, f32[704,11264]{1,0:T(8,128)} %fusion.5, f32[704,11264]{1,0:T(8,128)} %fusion.6, ...), kind=kOutput, calls=%fused_computation.1 | convolution fusion | flops 3425697792 | bytes 258375680 | tf_op jit(solution)/shard_map/cond/branch_1_fun/dot_general | solution.py:26
  515.4 22.3 %compare_select_fusion = f32[704,11264]{1,0:T(8,128)} fusion(f32[704,11264]{1,0:T(8,128)} %get-tuple-element.18, s32[11264]{0:T(1024)} %copy-done.1, s32[704]{0:T(1024)S(1)} %copy-done.3), kind=kLoop, calls=%fused_computation.33 | loop fusion | flops 15859712 | bytes 63486720 | tf_op jit(solution)/shard_map/jit(_where)/select_n | solution.py:42
  (12 shorter events, 0.1 us)
Async XLA Ops:
  6.5 241.6 %all-gather.2.cloned.1.call-start = ((), (), s32[]{:S(2)}) async-start(), calls=%async_computation | async-start | bytes 49020928 | tf_op jit(solution)/shard_map/all_gather | solution.py:53
  20.4 227.7 %copy-start.1 = (s32[11264]{0:T(1024)}, s32[11264]{0:T(1024)S(1)}, u32[]{:S(2)}) copy-start(s32[11264]{0:T(1024)S(1)} %reshape.22) | copy-start | bytes 135172
  20.5 0.6 copy-start.2
  248.2 267.2 %copy-start.3 = (s32[704]{0:T(1024)S(1)}, s32[704]{0:T(1024)}, u32[]{:S(2)}) copy-start(s32[704]{0:T(1024)} %copy-done.2) | copy-start | bytes 8452
  248.2 56.2 %copy-start = (bf16[8,192,704]{2,1,0:T(8,128)(2,1)S(1)}, bf16[8,192,704]{2,1,0:T(8,128)(2,1)}, u32[]{:S(2)}) copy-start(bf16[8,192,704]{2,1,0:T(8,128)(2,1)} %get-tuple-element.12) | copy-start | bytes 6488068 | tf_op jit(solution)/shard_map/cond
Sparse Core Ops, SparseCore 0:
  19.7 228.3 all-gather.1
where the time goes:
time: 555 us; the launch traced here: 545 us
  waiting for transfers between devices  222 us (40%)
  matrix products  211 us (38%)
  local copies, waits for them, and re-layouts  65.7 us (12%)
  other arithmetic  32.2 us (6%)
  between operations  14.6 us (3%)
    all_gather x1, waiting for transfers between devices, on_device(): lax.all_gather(normalized, 'blk', axis=2, tiled=True)  222 us
    dot_general x8, matrix products, fisher_sum(): lax.dot_general(left[subject], right[subject], (((0,), (0,)), ((), ())),...  211 us
    another operation x1, local copies, waits for them, and re-layouts  56.2 us
    select_n x1, other arithmetic, fisher_tile(): return jnp.where(same, total, empty)  22.3 us
  transfers between devices with their start and end apart: 1, of which 1 were waited for; matrix products, arithmetic and copies ran while one was open for 1% of the time, Pallas kernels for 0%

commit v1 on v0

v1 whole, which is shorter than its diff:
```python
import functools
import math

import jax
import jax.numpy as jnp
from jax import lax
from jax.experimental import pallas as pl
from jax.experimental.pallas import tpu as pltpu
from jax.sharding import PartitionSpec as P

USE_KERNEL_GATHER = True
LIMIT = 0.999


def normalize(chosen):
    values = chosen.astype(jnp.float32)
    center = values - jnp.mean(values, axis=1, keepdims=True)
    spread = jnp.mean(center * center, axis=1, keepdims=True)
    return (center / jnp.sqrt(spread + 1e-05)).astype(jnp.bfloat16)


def fisher_sum(left, right):
    frames = left.shape[1]
    total = jnp.zeros((left.shape[2], right.shape[2]), jnp.float32)
    for subject in range(left.shape[0]):
        corr = (
            lax.dot_general(
                left[subject],
                right[subject],
                (((0,), (0,)), ((), ())),
                preferred_element_type=jnp.float32,
            )
            / frames
        )
        clipped = jnp.clip(corr, -LIMIT, LIMIT)
        total = total + 0.5 * jnp.log((1.0 + clipped) / (1.0 - clipped))
    return total


def plain(series, subject_ids, net_labels):
    normalized = normalize(jnp.take(series, subject_ids, axis=0))
    rows = normalized.shape[2]
    index = lax.axis_index("blk")
    count = lax.axis_size("blk")
    row_labels = jnp.repeat(net_labels, count * rows // net_labels.shape[0])
    own_labels = lax.dynamic_slice_in_dim(row_labels, index * rows, rows)
    gathered = lax.all_gather(normalized, "blk", axis=2, tiled=True)
    same = own_labels[:, None] == row_labels[None, :]
    return jnp.where(same, fisher_sum(normalized, gathered), 0.0)


def normalize_kernel(ids_ref, me_ref, series_ref, out_ref, turned_ref):
    values = series_ref[0].astype(jnp.float32)
    frames = values.shape[0]
    center = values - jnp.sum(values, axis=0, keepdims=True) / frames
    spread = jnp.sum(center * center, axis=0, keepdims=True) / frames
    result = center / jnp.sqrt(spread + 1e-05)
    out_ref[0, 0] = result.astype(jnp.bfloat16)
    turned_ref[0] = result.T.astype(jnp.bfloat16)


def normalized_blocks(series, subject_ids, me, slots):
    _, frames, width = series.shape
    subjects = subject_ids.shape[0]
    return pl.pallas_call(
        normalize_kernel,
        grid_spec=pltpu.PrefetchScalarGridSpec(
            num_scalar_prefetch=2,
            grid=(subjects,),
            in_specs=[pl.BlockSpec((1, frames, width), lambda s, ids, me: (ids[s], 0, 0))],
            out_specs=[
                pl.BlockSpec((1, 1, frames, width), lambda s, ids, me: (me[0], s, 0, 0)),
                pl.BlockSpec((1, width, frames), lambda s, ids, me: (s, 0, 0)),
            ],
        ),
        out_shape=[
            jax.ShapeDtypeStruct((slots, subjects, frames, width), jnp.bfloat16),
            jax.ShapeDtypeStruct((subjects, width, frames), jnp.bfloat16),
        ],
        name="normalize",
    )(subject_ids, me, series)


def gather_kernel(count, chunks, in_ref, out_ref, send_sem, recv_sem):
    tall = count // 4
    me = lax.axis_index("blk")
    z = me // 4
    x = (me // 2) % 2
    c = me % 2
    per = out_ref.shape[1] // chunks
    UP, DOWN, SIDE, TWIN = range(4)
    half = chunks // 2

    def device(zz, xx, cc):
        return (zz * 2 + xx) * 2 + cc

    target = {
        UP: device(jnp.minimum(z + 1, tall - 1), x, c),
        DOWN: device(jnp.maximum(z - 1, 0), x, c),
        SIDE: device(z, 1 - x, c),
        TWIN: device(z, x, 1 - c),
    }
    has_up, has_down = z + 1 < tall, z > 0

    barrier = pltpu.get_barrier_semaphore()

    def greet(way):
        pl.semaphore_signal(
            barrier, inc=1, device_id={"blk": target[way]}, device_id_type=pl.DeviceIdType.MESH
        )

    greet(SIDE)
    greet(TWIN)
    pl.when(has_up)(lambda: greet(UP))
    pl.when(has_down)(lambda: greet(DOWN))
    pl.semaphore_wait(barrier, 2 + has_up.astype(jnp.int32) + has_down.astype(jnp.int32))

    def copy(way, block, q):
        part = out_ref.at[block, pl.ds(q * per, per)]
        return pltpu.make_async_remote_copy(
            src_ref=part,
            dst_ref=part,
            send_sem=send_sem.at[way, block, q],
            recv_sem=recv_sem.at[block, q],
            device_id={"blk": target[way]},
            device_id_type=pl.DeviceIdType.MESH,
        )

    def send(way, block, q):
        copy(way, block, q).start()

    def arrived(block, q):
        copy(TWIN, block, q).wait_recv()

    def by_side(zz, at, q):
        if q < half:
            return jnp.bool_(True)
        low = jnp.logical_and(zz == 0, at > 0)
        high = jnp.logical_and(zz == tall - 1, at < tall - 1)
        return jnp.logical_not(jnp.logical_or(low, high))

    for q in range(chunks):
        pl.when(has_up)(lambda: send(UP, me, q))
        pl.when(has_down)(lambda: send(DOWN, me, q))
        pl.when(by_side(z, z, q))(lambda: send(SIDE, me, q))
        send(TWIN, me, q)

    def step(k, carry):
        for q in range(chunks):

            @pl.when(z - k >= 0)
            def _():
                block = device(z - k, x, c)
                arrived(block, q)
                pl.when(has_up)(lambda: send(UP, block, q))
                pl.when(by_side(z - k, z, q))(lambda: send(SIDE, block, q))
                send(TWIN, block, q)

            @pl.when(z + k < tall)
            def _():
                block = device(z + k, x, c)
                arrived(block, q)
                pl.when(has_down)(lambda: send(DOWN, block, q))
                pl.when(by_side(z + k, z, q))(lambda: send(SIDE, block, q))
                send(TWIN, block, q)

            if q >= half:

                @pl.when(jnp.logical_and(z - k == -1, has_down))
                def _():
                    block = device(0, 1 - x, c)
                    arrived(block, q)
                    pl.when(has_up)(lambda: send(UP, block, q))
                    send(TWIN, block, q)

                @pl.when(jnp.logical_and(z + k == tall, has_up))
                def _():
                    block = device(tall - 1, 1 - x, c)
                    arrived(block, q)
                    pl.when(has_down)(lambda: send(DOWN, block, q))
                    send(TWIN, block, q)

            @pl.when(k == 1)
            def _():
                block = device(z, 1 - x, c)
                arrived(block, q)
                if q >= half:
                    pl.when(jnp.logical_and(z == 0, has_up))(lambda: send(UP, block, q))
                    pl.when(jnp.logical_and(z == tall - 1, has_down))(lambda: send(DOWN, block, q))
                send(TWIN, block, q)

            low = z - k + 1

            @pl.when(jnp.logical_and(jnp.logical_and(k > 1, low >= 0), by_side(low, z, q)))
            def _():
                block = device(low, 1 - x, c)
                arrived(block, q)
                send(TWIN, block, q)

            high = z + k - 1

            @pl.when(jnp.logical_and(jnp.logical_and(k > 1, high < tall), by_side(high, z, q)))
            def _():
                block = device(high, 1 - x, c)
                arrived(block, q)
                send(TWIN, block, q)

        return carry

    lax.fori_loop(1, tall + 1, step, 0)

    def finish(zz, carry):
        for q in range(chunks):
            own = device(zz, x, c)
            other = device(zz, 1 - x, c)
            arrived(device(zz, x, 1 - c), q)
            arrived(device(zz, 1 - x, 1 - c), q)
            copy(TWIN, own, q).wait_send()
            copy(TWIN, other, q).wait_send()
            pl.when(by_side(zz, z, q))(lambda: copy(SIDE, own, q).wait_send())
            pl.when(jnp.logical_and(has_up, zz <= z))(lambda: copy(UP, own, q).wait_send())
            pl.when(jnp.logical_and(has_down, zz >= z))(lambda: copy(DOWN, own, q).wait_send())
            if q >= half:
                pl.when(jnp.logical_and(has_up, zz == 0))(
                    lambda: copy(UP, other, q).wait_send()
                )
                pl.when(jnp.logical_and(has_down, zz == tall - 1))(
                    lambda: copy(DOWN, other, q).wait_send()
                )
        return carry

    lax.fori_loop(0, tall, finish, 0)


def gather(blocks, count):
    subjects = blocks.shape[1]
    chunks = math.gcd(subjects, 4)
    return pl.pallas_call(
        functools.partial(gather_kernel, count, chunks),
        out_shape=jax.ShapeDtypeStruct(blocks.shape, blocks.dtype),
        in_specs=[pl.BlockSpec(memory_space=pl.ANY)],
        out_specs=pl.BlockSpec(memory_space=pl.ANY),
        scratch_shapes=[
            pltpu.SemaphoreType.DMA((4, count, chunks)),
            pltpu.SemaphoreType.DMA((count, chunks)),
        ],
        input_output_aliases={0: 0},
        compiler_params=pltpu.CompilerParams(collective_id=0, has_side_effects=True),
        name="gather",
    )(blocks)


def fisher_kernel(rows, group, fetch_ref, match_ref, left_ref, right_ref, out_ref, pair):
    step = pl.program_id(0)
    subjects, width, frames = left_ref.shape
    first, second = match_ref[2 * step], match_ref[2 * step + 1]
    low = width // 128 * 128
    high = (width + 127) // 128 * 128
    bound = LIMIT * frames

    @pl.when(first + second == 0)
    def _():
        out_ref[...] = jnp.zeros_like(out_ref)

    @pl.when(first + second > 0)
    def _():
        for s in range(subjects):
            pair[s, :, :width] = right_ref[0, s]
            pair[s, :, width:] = right_ref[1, s]

    def tile(start, size, wanted, mixed):
        @pl.when(jnp.logical_and(wanted == 0, first + second > 0))
        def _():
            out_ref[:, start : start + size] = jnp.zeros((width, size), jnp.float32)

        @pl.when(wanted > 0)
        def _():
            def body(r, carry):
                at = pl.ds(pl.multiple_of(r * rows, rows), rows)
                total = None
                for g in range(0, subjects, group):
                    over = under = None
                    for s in range(g, min(g + group, subjects)):
                        dot = jnp.dot(
                            left_ref[s, at, :],
                            pair[s, :, start : start + size],
                            preferred_element_type=jnp.float32,
                        )
                        dot = jnp.clip(dot, -bound, bound)
                        plus, minus = frames + dot, frames - dot
                        over = plus if over is None else over * plus
                        under = minus if under is None else under * minus
                    term = 0.5 * jnp.log(over / under)
                    total = term if total is None else total + term
                if mixed:
                    lane = start + lax.broadcasted_iota(jnp.int32, total.shape, 1)
                    keep = jnp.where(lane < width, first, second)
                    total = jnp.where(keep > 0, total, 0.0)
                out_ref[at, start : start + size] = total
                return carry

            lax.fori_loop(0, width // rows, body, 0)

    for start in range(0, low, 256):
        tile(start, min(256, low - start), first, False)
    if high > low:
        tile(low, high - low, first + second, True)
    for start in range(high, 2 * width, 256):
        tile(start, min(256, 2 * width - start), second, False)


def correlate(left, blocks, match):
    count, subjects, frames, width = blocks.shape
    pairs = count // 2
    wanted = jnp.max(match.reshape(pairs, 2), axis=1)
    index = jnp.arange(pairs)
    latest = jnp.max(jnp.where((index[None, :] <= index[:, None]) & (wanted[None, :] > 0), index[None, :], 0), axis=1)
    group = max(1, int(30 / math.log10(2 * frames)))
    rows = math.gcd(width, 64)
    return pl.pallas_call(
        functools.partial(fisher_kernel, rows, group),
        grid_spec=pltpu.PrefetchScalarGridSpec(
            num_scalar_prefetch=2,
            grid=(pairs,),
            in_specs=[
                pl.BlockSpec((subjects, width, frames), lambda p, fetch, match: (0, 0, 0)),
                pl.BlockSpec((2, subjects, frames, width), lambda p, fetch, match: (fetch[p], 0, 0, 0)),
            ],
            out_specs=pl.BlockSpec((width, 2 * width), lambda p, fetch, match: (0, p)),
            scratch_shapes=[pltpu.VMEM((subjects, frames, 2 * width), jnp.bfloat16)],
        ),
        out_shape=jax.ShapeDtypeStruct((width, count * width), jnp.float32),
        compiler_params=pltpu.CompilerParams(vmem_limit_bytes=60 * 1024 * 1024),
        name="correlate",
    )(latest.astype(jnp.int32), match, left, blocks)


def on_device(series, subject_ids, net_labels):
    count = lax.axis_size("blk")
    width = series.shape[2]
    fits = net_labels.shape[0] == count and count % 4 == 0 and 2 * width % 128 == 0
    if not fits:
        return plain(series, subject_ids, net_labels)
    me = lax.axis_index("blk").astype(jnp.int32)
    match = (net_labels == net_labels[me]).astype(jnp.int32)
    if USE_KERNEL_GATHER:
        blocks, left = normalized_blocks(series, subject_ids, me[None], count)
        blocks = gather(blocks, count)
    else:
        own, left = normalized_blocks(series, subject_ids, jnp.zeros((1,), jnp.int32), 1)
        blocks = lax.all_gather(own, "blk", axis=0, tiled=True)
    return correlate(left, blocks, match)


def solution(mesh):
    return jax.shard_map(
        on_device,
        mesh=mesh,
        in_specs=(P(None, None, "blk"), P("parts"), P()),
        out_specs=P(("parts", "blk"), None),
        check_vma=False,
    )
```

time: 555 us -> 284 us (0.51); the launches traced: 545 us -> 288 us
  Pallas kernels: 0 us -> 284 us
  waiting for transfers between devices: 222 us -> 0 us
  matrix products: 211 us -> 0 us
  local copies, waits for them, and re-layouts: 65.7 us -> 1.4 us
  other arithmetic: 32.2 us -> 2.17 us
  between operations: 14.6 us -> 0.02 us
    pallas_call x0 -> x3, Pallas kernels: none -> 284 us  [the longest x1 187 us: gather(): pl.pallas_call(functools.partial(gather_kernel, count, chunks), out_shape...]
    all_gather x1 -> x0, waiting for transfers between devices: 222 us -> none  [on_device(): lax.all_gather(normalized, 'blk', axis=2, tiled=True)]
    dot_general x8 -> x0, matrix products: 211 us -> none  [fisher_sum(): lax.dot_general(left[subject], right[subject], (((0,), (0,)), ((), ())),...]
    another operation x1 -> x0, local copies, waits for them, and re-layouts: 56.2 us -> none
    select_n x2 -> x0, other arithmetic: 22.9 us -> none  [the longest x1 22.3 us: fisher_tile(): return jnp.where(same, total, empty)]
  transfers between devices with their start and end apart: 1 -> 0, of which waited for: 1 -> 0; matrix products, arithmetic and copies ran while one was open for 1% -> 0% of each run, Pallas kernels for 0% -> 0%
where the time goes in v1:
time: 284 us; the launch traced here: 288 us
  Pallas kernels  284 us (100%)
    pallas_call x1, Pallas kernels, gather(): pl.pallas_call(functools.partial(gather_kernel, count, chunks), out_shape...  187 us
    pallas_call x1, Pallas kernels, correlate(): pl.pallas_call(functools.partial(fisher_kernel, rows, group), grid_spec=p...  89.7 us
    pallas_call x1, Pallas kernels, normalized_blocks(): pl.pallas_call(normalize_kernel, grid_spec=pltpu.PrefetchScalarGridSpec(n...  7.79 us

profile of v1, /device:TPU:7, one launch (start us, length us, event | category | flops | bytes accessed | tf_op | source)
XLA Modules:
  0.0 288.0 jit_solution(927715236286161533)
XLA Ops:
  0.0 1.3 dynamic_slice.3
  1.3 1.3 compare_convert_fusion.match_ref
  2.7 0.0 copy-start
  2.7 0.1 reshape.7
  2.7 0.1 reduce_max.18
  2.9 0.7 select_reduce_fusion.fetch_ref
  3.6 7.8 %normalize.1 = (bf16[16,8,192,704]{3,2,1,0:T(8,128)(2,1)}, bf16[8,704,192]{2,1,0:T(8,128)(2,1)}) custom-call(s32[8]{0:T(128)} %ids_ref.1, s32[1]{0:T(128)} %bitcast.1.me_ref, bf16[16,192,704]{2,1,0:T(8,128)(2,1)} %series_ref.1), custom_call_target="tpu_custom_call" | custom-call | tf_op jit(solution)/shard_map/normalize/pallas_call | solution.py:65
  11.4 187.0 %gather.1.right_ref = bf16[16,8,192,704]{3,2,1,0:T(8,128)(2,1)} custom-call(bf16[16,8,192,704]{3,2,1,0:T(8,128)(2,1)} %get-tuple-element.8.in_ref), custom_call_target="tpu_custom_call", output_to_operand_aliasing={{}: (0, {})} | custom-call | tf_op jit(solution)/shard_map/gather/pallas_call | solution.py:238
  198.3 0.0 copy-done
  198.3 89.7 %correlate.1 = f32[704,11264]{1,0:T(8,128)} custom-call(s32[8]{0:T(128)} %select_reduce_fusion.fetch_ref, s32[16]{0:T(128)} %copy-done, bf16[8,704,192]{2,1,0:T(8,128)(2,1)} %get-tuple-element.7.left_ref, bf16[16,8,192,704]{3,2,1,0:T(8,128)(2,1)} %gather.1.right_ref), custom_call_target="tpu_custom_call" | custom-call | tf_op jit(solution)/shard_map/correlate/pallas_call | solution.py:320
  (1 shorter events, 0.0 us)
Async XLA Ops:
  2.7 195.7 %copy-start = (s32[16]{0:T(128)}, s32[16]{0:T(128)S(1)}, u32[]{:S(2)}) copy-start(s32[16]{0:T(128)S(1)} %compare_convert_fusion.match_ref) | copy-start | bytes 196
